TPU v7x, 256 devices: a whole 4x4x8 slice. The times are simulated.
256 devices in a mesh: row: 16 (over y, x), col: 2 (over core), ctx: 8 (over z).
Axes of the slice: x: 4, y: 4, z: 8, core: 2. Of those that a mesh axis runs over, the one named last changes fastest.
Arguments:
- queries: bfloat16 [8192, 6144], P(('col', 'ctx'), 'row'), may hold values from -16 to 16
- keys: bfloat16 [8192, 6144], P(('col', 'ctx'), 'row'), may hold values from -16 to 16
- values: bfloat16 [8192, 6144], P(('col', 'ctx'), 'row'), may hold values from -6 to 6
- out_weight: bfloat16 [6144, 6144], P('col', 'row'), may hold values from -0.078125 to 0.078125
- cotangent: bfloat16 [8192, 6144], P(('col', 'ctx'), 'row'), may hold values from -0.125 to 0.125
- block_mask: int32 [16, 16], replicated, may hold values from 0 to 1, as said below
Outputs:
- mixed_out: bfloat16 [8192, 6144], P(('col', 'ctx'), 'row')
- grad_weight: bfloat16 [6144, 6144], P(('col', 'ctx'), 'row')
Inputs may be any that keep to these rules, and one draw needn't show every extreme that they name: block_mask[i, i] is 1 for every block i, and block_mask[i, j] is 0 for j > i.
All inputs are finite; a program needn't handle non-finite values.
Results may differ from a plain program's by a relative error of at most 0.013.
Values may be sent and summed in bfloat16 or wider, within the bound.
A program may use at most 64 MiB of HBM per device.

v0:
```python
import math
import jax
import jax.numpy as jnp
from jax import lax
from jax.sharding import PartitionSpec as P

HD = 128
BLOCK = 512
NEGATIVE_FILL = -1e30


def attend_block(carried, query_heads, key_block, value_block, allowed, score_scale):
    run_max, run_sum, weighted = carried
    tok_rows, head_count, head_size = query_heads.shape
    key_heads = key_block.reshape(key_block.shape[0], head_count, head_size)
    value_heads = value_block.reshape(value_block.shape[0], head_count, head_size)
    scores = (
        jnp.einsum("thd,uhd->thu", query_heads, key_heads, preferred_element_type=jnp.float32)
        * score_scale
    )
    scores = jnp.where(allowed[:, None, None], scores, NEGATIVE_FILL)
    new_max = jnp.maximum(run_max, jnp.max(scores, axis=2))
    correction = jnp.exp(run_max - new_max)
    weights = jnp.where(allowed[:, None, None], jnp.exp(scores - new_max[:, :, None]), 0.0)
    new_sum = run_sum * correction + jnp.sum(weights, axis=2)
    product = jnp.einsum(
        "thu,uhd->thd",
        weights.astype(jnp.bfloat16),
        value_heads,
        preferred_element_type=jnp.float32,
    )
    new_weighted = weighted * correction[:, :, None] + product
    return (new_max, new_sum, new_weighted)


def body(queries, keys, values, out_weight, cotangent, block_mask):
    tok_rows, feature_width = queries.shape
    head_count = feature_width // HD
    query_heads = queries.reshape(tok_rows, head_count, HD)
    score_scale = 1.0 / math.sqrt(HD)
    local_blocks = tok_rows // BLOCK
    first_block = lax.axis_index(("col", "ctx")) * local_blocks
    local_mask = lax.dynamic_slice_in_dim(block_mask, first_block, local_blocks, 0)
    start_state = (
        jnp.full((tok_rows, head_count), NEGATIVE_FILL, jnp.float32),
        jnp.zeros((tok_rows, head_count), jnp.float32),
        jnp.zeros((tok_rows, head_count, HD), jnp.float32),
    )
    key_piece = lax.all_gather(keys, ("col", "ctx"), axis=0, tiled=True)
    value_piece = lax.all_gather(values, ("col", "ctx"), axis=0, tiled=True)
    block_count = key_piece.shape[0] // BLOCK
    key_stack = key_piece.reshape(block_count, BLOCK, feature_width)
    value_stack = value_piece.reshape(block_count, BLOCK, feature_width)
    block_columns = jnp.arange(block_count, dtype=jnp.int32)

    def one_block(state_in, entries):
        key_block, value_block, block_column = entries
        mask_column = lax.dynamic_index_in_dim(local_mask, block_column, 1, keepdims=False)
        allowed = jnp.repeat(mask_column, BLOCK, total_repeat_length=tok_rows) == 1
        updated = attend_block(state_in, query_heads, key_block, value_block, allowed, score_scale)
        return (updated, None)

    state_out, _ = lax.scan(one_block, start_state, (key_stack, value_stack, block_columns))
    run_max, run_sum, weighted = state_out
    attended = (
        (weighted / run_sum[:, :, None]).reshape(tok_rows, feature_width).astype(jnp.bfloat16)
    )
    all_heads = lax.all_gather(attended, "row", axis=1, tiled=True)
    head_columns = all_heads
    mixed_out = jnp.dot(
        head_columns,
        lax.all_gather(out_weight, "col", axis=0, tiled=True),
        preferred_element_type=jnp.float32,
    )
    head_columns = all_heads
    grad_weight = lax.psum_scatter(
        lax.dot_general(
            head_columns, cotangent, (((0,), (0,)), ((), ())), preferred_element_type=jnp.float32
        ),
        ("col", "ctx"),
        scatter_dimension=0,
        tiled=True,
    )
    return (mixed_out.astype(jnp.bfloat16), grad_weight.astype(jnp.bfloat16))


def solution(mesh):
    in_specs = (
        P(("col", "ctx"), "row"),
        P(("col", "ctx"), "row"),
        P(("col", "ctx"), "row"),
        P("col", "row"),
        P(("col", "ctx"), "row"),
        P(),
    )
    out_specs = (P(("col", "ctx"), "row"), P(("col", "ctx"), "row"))
    return jax.shard_map(body, mesh=mesh, in_specs=in_specs, out_specs=out_specs, check_vma=False)
```

profile of v0, /device:TPU:1, one launch (start us, length us, event | category | flops | bytes accessed | tf_op | source)
XLA Modules:
  0.0 622.6 jit_solution(9049366893125646251)
XLA Ops:
  12.0 48.1 %all-gather.5.cloned.1.call-done = bf16[8192,384]{1,0:T(8,128)(2,1)} async-done(((bf16[512,384]{1,0:T(8,128)(2,1)}), bf16[8192,384]{1,0:T(8,128)(2,1)}) %all-gather.5.cloned.1.call-update) | async-done | bytes 6291472 | tf_op jit(solution)/shard_map/all_gather | solution.py:49
  60.1 46.5 %all-gather.7.cloned.1.call-done = bf16[8192,384]{1,0:T(8,128)(2,1)} async-done(((bf16[512,384]{1,0:T(8,128)(2,1)}), bf16[8192,384]{1,0:T(8,128)(2,1)}) %all-gather.7.cloned.1.call-update) | async-done | bytes 6291472 | tf_op jit(solution)/shard_map/all_gather | solution.py:50
  107.2 304.6 %while.22 = (s32[]{:T(128)}, f32[512,3]{0,1:T(4,128)}, f32[512,3]{0,1:T(4,128)}, f32[512,3,128]{0,2,1:T(8,128)}, s32[16]{0:T(128)}, /*index=5*/s32[1,16]{1,0:T(1...) while((s32[]{:T(128)}, f32[512,3]{0,1:T(4,128)}, ...), condition=%wide.region_3.4_spmd.clone, body=%wide.region_0.3_spmd.clone.sunk | while | flops 413474304 | bytes 15433919 | solution.py:63
  114.3 2.4 bitcast_reduce_fusion.2
  120.7 3.4 fusion.42
  131.8 2.4 bitcast_reduce_fusion.2
  139.5 3.7 fusion.42
  151.0 2.4 bitcast_reduce_fusion.2
  158.7 3.7 fusion.42
  177.8 3.7 fusion.42
  189.2 2.4 bitcast_reduce_fusion.2
  197.0 3.7 fusion.42
  208.4 2.4 bitcast_reduce_fusion.2
  216.1 3.7 fusion.42
  235.2 3.7 fusion.42
  254.4 3.7 fusion.42
  265.8 2.4 bitcast_reduce_fusion.2
  273.5 3.7 fusion.42
  292.7 3.7 fusion.42
  311.8 3.7 fusion.42
  323.2 2.4 bitcast_reduce_fusion.2
  330.9 3.7 fusion.42
  350.1 3.7 fusion.42
  361.5 2.4 bitcast_reduce_fusion.2
  369.2 3.7 fusion.42
  388.3 3.7 fusion.42
  407.5 3.7 fusion.42
  414.4 64.1 %all-gather.9.cloned.1.call-done = bf16[512,6144]{0,1:T(8,128)(2,1)} async-done(((bf16[512,384]{0,1:T(8,128)(2,1)}), bf16[512,6144]{0,1:T(8,128)(2,1)}) %all-gather.9.cloned.1.call-update) | async-done | bytes 6291472 | tf_op jit(solution)/shard_map/all_gather | solution.py:68
  478.5 9.9 %fusion.19 = f32[6144,384]{1,0:T(8,128)} fusion(bf16[512,6144]{0,1:T(8,128)(2,1)} %all-gather.9.cloned.1.call-done, bf16[512,384]{1,0:T(8,128)(2,1)S(1)} %copy-done), kind=kOutput, calls=%fused_computation.27 | convolution fusion | flops 2415919104 | bytes 16121856 | tf_op jit(solution)/shard_map/dot_general | solution.py:77
  488.4 12.0 %all-gather.11.cloned.1.call-done = bf16[6144,384]{1,0:T(8,128)(2,1)} async-done(((bf16[3072,384]{1,0:T(8,128)(2,1)}), bf16[6144,384]{1,0:T(8,128)(2,1)}) %all-gather.11.cloned.1.call-update) | async-done | bytes 4718608 | tf_op jit(solution)/shard_map/all_gather | solution.py:72
  500.4 8.3 %convolution_convert_fusion = bf16[512,384]{1,0:T(8,128)(2,1)} fusion(bf16[512,6144]{0,1:T(8,128)(2,1)} %all-gather.9.cloned.1.call-done, bf16[6144,384]{1,0:T(8,128)(2,1)} %all-gather.11.cloned.1.call-done), kind=kOutput, calls=%fused_computation.23 | convolution fusion | flops 2416115712 | bytes 11403264 | tf_op jit(solution)/shard_map/dot_general | solution.py:70
  508.7 105.5 %reduce-scatter.2.cloned.1.call-done = f32[384,384]{1,0:T(8,128)} async-done(((f32[6144,384]{1,0:T(8,128)}), f32[384,384]{1,0:T(8,128)}) %reduce-scatter.2.cloned.1.call-update) | async-done | bytes 589840 | tf_op jit(solution)/shard_map/reduce_scatter | solution.py:76
  (173 shorter events, 206.9 us)
Async XLA Ops:
  7.2 471.3 %copy-start = (bf16[512,384]{1,0:T(8,128)(2,1)S(1)}, bf16[512,384]{1,0:T(8,128)(2,1)}, u32[]{:S(2)}) copy-start(bf16[512,384]{1,0:T(8,128)(2,1)} %param.16) | copy-start | bytes 1179652
  7.2 53.0 %all-gather.5.cloned.1.call-start = ((), (), s32[]{:S(2)}) async-start(), calls=%async_computation.1 | async-start | bytes 6684672 | tf_op jit(solution)/shard_map/all_gather | solution.py:49
  7.9 98.7 %all-gather.7.cloned.1.call-start = ((), (), s32[]{:S(2)}) async-start(), calls=%async_computation.2 | async-start | bytes 6684672 | tf_op jit(solution)/shard_map/all_gather | solution.py:50
  8.7 469.8 %all-gather.9.cloned.1.call-start = ((), (), s32[]{:S(2)}) async-start(), calls=%async_computation.3 | async-start | bytes 6684672 | tf_op jit(solution)/shard_map/all_gather | solution.py:68
  413.7 86.7 %all-gather.11.cloned.1.call-start = ((), (), s32[]{:S(2)}) async-start(), calls=%async_computation.4 | async-start | bytes 7077888 | tf_op jit(solution)/shard_map/all_gather | solution.py:72
  414.3 200.0 %reduce-scatter.2.cloned.1.call-start = ((), (), s32[]{:S(2)}) async-start(), calls=%async_computation.5 | async-start | bytes 10027008 | tf_op jit(solution)/shard_map/reduce_scatter | solution.py:76
Sparse Core Ops, SparseCore 0:
  9.8 50.2 all-gather.4
  62.0 44.6 all-gather.6
  413.9 64.5 all-gather.8
  480.1 20.2 all-gather.10
  502.8 111.4 reduce-scatter.1
where the time goes:
time: 627 us; the launch traced here: 623 us
  waiting for transfers between devices  278 us (44%)
  matrix products  115 us (18%)
  local copies, waits for them, and re-layouts  110 us (18%)
  other arithmetic  75.8 us (12%)
  loops' own time  29.9 us (5%)
  between operations  13.8 us (2%)
    reduce_scatter x1, waiting for transfers between devices, body(): lax.psum_scatter(lax.dot_general(head_columns, cotangent, (((0,), (0,)),...  106 us
    dynamic_slice x64, local copies, waits for them, and re-layouts, body(): lax.scan(one_block, start_state, (key_stack, value_stack, block_columns))  96.5 us
    all_gather x1, waiting for transfers between devices, body(): all_heads = lax.all_gather(attended, 'row', axis=1, tiled=True)  64.1 us
    dot_general x16, matrix products, attend_block(): jnp.einsum('thu,uhd->thd', weights.astype(jnp.bfloat16), value_heads, pre...  58.4 us
    all_gather x1, waiting for transfers between devices, body(): key_piece = lax.all_gather(keys, ('col', 'ctx'), axis=0, tiled=True)  48.1 us
    all_gather x1, waiting for transfers between devices, body(): value_piece = lax.all_gather(values, ('col', 'ctx'), axis=0, tiled=True)  46.5 us
    dot_general x16, matrix products, attend_block(): jnp.einsum('thd,uhd->thu', query_heads, key_heads, preferred_element_type...  38.2 us
    another operation x1, loops' own time, body(): lax.scan(one_block, start_state, (key_stack, value_stack, block_columns))  29.9 us
  transfers between devices with their start and end apart: 5, of which 5 were waited for; matrix products, arithmetic and copies ran while one was open for 3% of the time, Pallas kernels for 0%

commit v1 on v0

--- a/solution.py
+++ b/solution.py
@@ -7,6 +7,22 @@
 HD = 128
 BLOCK = 512
 NEGATIVE_FILL = -1e30
+
+
+def gather_around(x, axis, dim):
+    ways, here, step = (lax.axis_size(axis), lax.axis_index(axis), x.shape[dim])
+    shape = [n * ways if d == dim else n for d, n in enumerate(x.shape)]
+    full = lax.dynamic_update_slice_in_dim(jnp.zeros(shape, x.dtype), x, here * step, axis=dim)
+    going_up = going_down = x
+    for far in range(1, ways // 2 + 1):
+        going_up = lax.ppermute(going_up, axis, [(d, (d + 1) % ways) for d in range(ways)])
+        full = lax.dynamic_update_slice_in_dim(full, going_up, (here - far) % ways * step, axis=dim)
+        if 2 * far < ways:
+            going_down = lax.ppermute(going_down, axis, [(d, (d - 1) % ways) for d in range(ways)])
+            full = lax.dynamic_update_slice_in_dim(
+                full, going_down, (here + far) % ways * step, axis=dim
+            )
+    return full
 
 
 def attend_block(carried, query_heads, key_block, value_block, allowed, score_scale):
@@ -46,7 +62,7 @@
         jnp.zeros((tok_rows, head_count), jnp.float32),
         jnp.zeros((tok_rows, head_count, HD), jnp.float32),
     )
-    key_piece = lax.all_gather(keys, ("col", "ctx"), axis=0, tiled=True)
+    key_piece = gather_around(keys, ("col", "ctx"), 0)
     value_piece = lax.all_gather(values, ("col", "ctx"), axis=0, tiled=True)
     block_count = key_piece.shape[0] // BLOCK
     key_stack = key_piece.reshape(block_count, BLOCK, feature_width)

time: 627 us -> 650 us (1.037)
  starting transfers between devices: 0.19 us -> 27.4 us
  waiting for transfers between devices: 278 us -> 257 us
  local copies, waits for them, and re-layouts: 110 us -> 127 us
    ppermute x0 -> x15, waiting for transfers between devices: none -> 76.4 us  [the longest x8 60.5 us: gather_around(): lax.ppermute(going_up, axis, [(d, (d + 1) % ways) for d in range(ways)])]
    all_gather x1 -> x0, waiting for transfers between devices: 48.1 us -> none  [body(): key_piece = lax.all_gather(keys, ('col', 'ctx'), axis=0, tiled=True)]
    all_gather x1, waiting for transfers between devices: 46.5 us -> 0.01 us  [body(): value_piece = lax.all_gather(values, ('col', 'ctx'), axis=0, tiled=True)]
    ppermute x0 -> x15, starting transfers between devices: none -> 27.3 us  [the longest x7 24.7 us: gather_around(): lax.ppermute(going_down, axis, [(d, (d - 1) % ways) for d in range(ways)])]
    dynamic_update_slice x0 -> x16, local copies, waits for them, and re-layouts: none -> 13.7 us  [the longest x8 7.38 us: gather_around(): lax.dynamic_update_slice_in_dim(full, going_up, (here - far) % ways * ste...]
  transfers between devices with their start and end apart: 5 -> 19, of which waited for: 5 -> 12; matrix products, arithmetic and copies ran while one was open for 3% -> 6% of each run, Pallas kernels for 0% -> 0%
where the time goes in v1:
time: 650 us; the launch traced here: 646 us
  waiting for transfers between devices  257 us (40%)
  local copies, waits for them, and re-layouts  127 us (20%)
  matrix products  114 us (18%)
  other arithmetic  74.8 us (12%)
  loops' own time  31.4 us (5%)
  starting transfers between devices  27.4 us (4%)
  between operations  13.8 us (2%)
    reduce_scatter x1, waiting for transfers between devices, body(): lax.psum_scatter(lax.dot_general(head_columns, cotangent, (((0,), (0,)),...  106 us
    dynamic_slice x64, local copies, waits for them, and re-layouts, body(): lax.scan(one_block, start_state, (key_stack, value_stack, block_columns))  97.1 us
    all_gather x1, waiting for transfers between devices, body(): all_heads = lax.all_gather(attended, 'row', axis=1, tiled=True)  61.6 us
    ppermute x8, waiting for transfers between devices, gather_around(): lax.ppermute(going_up, axis, [(d, (d + 1) % ways) for d in range(ways)])  60.5 us
    dot_general x16, matrix products, attend_block(): jnp.einsum('thu,uhd->thd', weights.astype(jnp.bfloat16), value_heads, pre...  57.9 us
    dot_general x16, matrix products, attend_block(): jnp.einsum('thd,uhd->thu', query_heads, key_heads, preferred_element_type...  37.4 us
    another operation x1, loops' own time, body(): lax.scan(one_block, start_state, (key_stack, value_stack, block_columns))  31.4 us
    ppermute x7, starting transfers between devices, gather_around(): lax.ppermute(going_down, axis, [(d, (d - 1) % ways) for d in range(ways)])  24.7 us
  transfers between devices with their start and end apart: 19, of which 12 were waited for; matrix products, arithmetic and copies ran while one was open for 6% of the time, Pallas kernels for 0%

profile of v1, /device:TPU:1, one launch (start us, length us, event | category | flops | bytes accessed | tf_op | source)
XLA Modules:
  0.0 645.5 jit_solution(2379721795635148108)
XLA Ops:
  10.5 4.6 collective-permute-start.1
  15.1 8.9 %collective-permute-done = bf16[512,384]{1,0:T(8,128)(2,1)S(1)} collective-permute-done((bf16[512,384]{1,0:T(8,128)(2,1)}, bf16[512,384]{1,0:T(8,128)(2,1)S(1)}, u32[]{:S(2)}, u32[]{:S(2)}) %collective-permute-start) | collective-permute-done | bytes 393248 | tf_op jit(solution)/shard_map/ppermute | solution.py:18
  24.4 3.6 collective-permute-start.3
  27.9 16.4 %collective-permute-done.2 = bf16[512,384]{1,0:T(8,128)(2,1)S(1)} collective-permute-done((bf16[512,384]{1,0:T(8,128)(2,1)S(1)}, bf16[512,384]{1,0:T(8,128)(2,1)S(1)}, u32[]{:S(2)}, u32[]{:S(2)}) %collective-permute-start.2) | collective-permute-done | bytes 393248 | tf_op jit(solution)/shard_map/ppermute | solution.py:18
  47.3 17.5 %collective-permute-done.4 = bf16[512,384]{1,0:T(8,128)(2,1)S(1)} collective-permute-done((bf16[512,384]{1,0:T(8,128)(2,1)S(1)}, bf16[512,384]{1,0:T(8,128)(2,1)S(1)}, u32[]{:S(2)}, u32[]{:S(2)}) %collective-permute-start.4) | collective-permute-done | bytes 393248 | tf_op jit(solution)/shard_map/ppermute | solution.py:18
  68.0 14.1 %collective-permute-done.6 = bf16[512,384]{1,0:T(8,128)(2,1)S(1)} collective-permute-done((bf16[512,384]{1,0:T(8,128)(2,1)S(1)}, bf16[512,384]{1,0:T(8,128)(2,1)S(1)}, u32[]{:S(2)}, u32[]{:S(2)}) %collective-permute-start.6) | collective-permute-done | bytes 393248 | tf_op jit(solution)/shard_map/ppermute | solution.py:18
  96.5 5.5 collective-permute-done.9
  101.9 3.7 collective-permute-start.11
  109.8 4.6 collective-permute-done.11
  114.5 3.7 collective-permute-start.13
  121.3 5.5 collective-permute-done.13
  132.5 304.3 %while.22 = (s32[]{:T(128)}, f32[512,3]{0,1:T(4,128)}, f32[512,3]{0,1:T(4,128)}, f32[512,3,128]{0,2,1:T(8,128)}, s32[16]{0:T(128)}, /*index=5*/s32[1,16]{1,0:T(1...) while((s32[]{:T(128)}, f32[512,3]{0,1:T(4,128)}, ...), condition=%wide.region_3.4_spmd.clone, body=%wide.region_0.3_spmd.clone.sunk | while | flops 413474304 | bytes 15433919 | solution.py:79
  164.8 3.6 fusion.42
  184.0 3.6 fusion.42
  203.1 3.6 fusion.42
  222.2 3.6 fusion.42
  241.3 3.6 fusion.42
  260.5 3.6 fusion.42
  279.6 3.6 fusion.42
  298.7 3.6 fusion.42
  317.8 3.6 fusion.42
  337.0 3.6 fusion.42
  356.1 3.6 fusion.42
  375.2 3.6 fusion.42
  394.3 3.6 fusion.42
  413.5 3.6 fusion.42
  432.6 3.6 fusion.42
  439.6 61.6 %all-gather.6.cloned.1.call-done = bf16[512,6144]{0,1:T(8,128)(2,1)} async-done(((bf16[512,384]{0,1:T(8,128)(2,1)}), bf16[512,6144]{0,1:T(8,128)(2,1)}) %all-gather.6.cloned.1.call-update) | async-done | bytes 6291472 | tf_op jit(solution)/shard_map/all_gather | solution.py:84
  501.2 9.9 %fusion.19 = f32[6144,384]{1,0:T(8,128)} fusion(bf16[512,6144]{0,1:T(8,128)(2,1)} %all-gather.6.cloned.1.call-done, bf16[512,384]{1,0:T(8,128)(2,1)S(1)} %copy-done), kind=kOutput, calls=%fused_computation.43 | convolution fusion | flops 2415919104 | bytes 16121856 | tf_op jit(solution)/shard_map/dot_general | solution.py:93
  511.1 12.2 %all-gather.8.cloned.1.call-done = bf16[6144,384]{1,0:T(8,128)(2,1)} async-done(((bf16[3072,384]{1,0:T(8,128)(2,1)}), bf16[6144,384]{1,0:T(8,128)(2,1)}) %all-gather.8.cloned.1.call-update) | async-done | bytes 4718608 | tf_op jit(solution)/shard_map/all_gather | solution.py:88
  523.3 8.3 %convolution_convert_fusion = bf16[512,384]{1,0:T(8,128)(2,1)} fusion(bf16[512,6144]{0,1:T(8,128)(2,1)} %all-gather.6.cloned.1.call-done, bf16[6144,384]{1,0:T(8,128)(2,1)} %all-gather.8.cloned.1.call-done), kind=kOutput, calls=%fused_computation.23 | convolution fusion | flops 2416115712 | bytes 11403264 | tf_op jit(solution)/shard_map/dot_general | solution.py:86
  531.6 105.5 %reduce-scatter.2.cloned.1.call-done = f32[384,384]{1,0:T(8,128)} async-done(((f32[6144,384]{1,0:T(8,128)}), f32[384,384]{1,0:T(8,128)}) %reduce-scatter.2.cloned.1.call-update) | async-done | bytes 589840 | tf_op jit(solution)/shard_map/reduce_scatter | solution.py:92
  (227 shorter events, 260.1 us)
Async XLA Ops:
  7.2 494.1 %copy-start = (bf16[512,384]{1,0:T(8,128)(2,1)S(1)}, bf16[512,384]{1,0:T(8,128)(2,1)}, u32[]{:S(2)}) copy-start(bf16[512,384]{1,0:T(8,128)(2,1)} %param.16) | copy-start | bytes 1179652
  7.2 81.5 %copy-start.1 = (bf16[512,384]{1,0:T(8,128)(2,1)S(1)}, bf16[512,384]{1,0:T(8,128)(2,1)}, u32[]{:S(2)}) copy-start(bf16[512,384]{1,0:T(8,128)(2,1)} %param.13) | copy-start | bytes 1179652
  7.2 124.7 %all-gather.4.cloned.1.call-start = ((), (), s32[]{:S(2)}) async-start(), calls=%async_computation.1 | async-start | bytes 6684672 | tf_op jit(solution)/shard_map/all_gather | solution.py:66
  7.9 493.3 %all-gather.6.cloned.1.call-start = ((), (), s32[]{:S(2)}) async-start(), calls=%async_computation.2 | async-start | bytes 6684672 | tf_op jit(solution)/shard_map/all_gather | solution.py:84
  8.0 16.1 %collective-permute-start = (bf16[512,384]{1,0:T(8,128)(2,1)}, bf16[512,384]{1,0:T(8,128)(2,1)S(1)}, u32[]{:S(2)}, u32[]{:S(2)}) collective-permute-start(bf16[512,384]{1,0:T(8,128)(2,1)} %param.13), channel_id=1, source_target_pairs={{0,1},{1,2},{2,3},{3,4},{4,5},{5,6},{6,7},{7,8},{8,9},{9,10},{10,1... | collective-permute-start | bytes 1179656 | tf_op jit(solution)/shard_map/ppermute | solution.py:18
  10.5 13.8 %collective-permute-start.1 = (bf16[512,384]{1,0:T(8,128)(2,1)}, bf16[512,384]{1,0:T(8,128)(2,1)S(1)}, u32[]{:S(2)}, u32[]{:S(2)}) collective-permute-start(bf16[512,384]{1,0:T(8,128)(2,1)} %param.13), channel_id=1, source_target_pairs={{0,15},{1,0},{2,1},{3,2},{4,3},{5,4},{6,5},{7,6},{8,7},{9,8},{10,9... | collective-permute-start | bytes 1179656 | tf_op jit(solution)/shard_map/ppermute | solution.py:21
  24.1 23.3 %copy-start.4 = (bf16[512,384]{1,0:T(8,128)(2,1)}, bf16[512,384]{1,0:T(8,128)(2,1)S(1)}, u32[]{:S(2)}) copy-start(bf16[512,384]{1,0:T(8,128)(2,1)S(1)} %collective-permute-done) | copy-start | bytes 1179652
  24.1 20.3 %collective-permute-start.2 = (bf16[512,384]{1,0:T(8,128)(2,1)S(1)}, bf16[512,384]{1,0:T(8,128)(2,1)S(1)}, u32[]{:S(2)}, u32[]{:S(2)}) collective-permute-start(bf16[512,384]{1,0:T(8,128)(2,1)S(1)} %collective-permute-done), channel_id=1, source_target_pairs={{0,1},{1,2},{2,3},{3,4},{4,5},{5,6},{6,7},{7,8},{8,9},{9,10},{10,1... | collective-permute-start | bytes 1179656 | tf_op jit(solution)/shard_map/ppermute | solution.py:18
  24.4 20.0 %collective-permute-start.3 = (bf16[512,384]{1,0:T(8,128)(2,1)S(1)}, bf16[512,384]{1,0:T(8,128)(2,1)S(1)}, u32[]{:S(2)}, u32[]{:S(2)}) collective-permute-start(bf16[512,384]{1,0:T(8,128)(2,1)S(1)} %collective-permute-done.1), channel_id=1, source_target_pairs={{0,15},{1,0},{2,1},{3,2},{4,3},{5,4},{6,5},{7,6},{8,7},{9,8},{10,9... | collective-permute-start | bytes 1179656 | tf_op jit(solution)/shard_map/ppermute | solution.py:21
  44.4 20.5 %collective-permute-start.4 = (bf16[512,384]{1,0:T(8,128)(2,1)S(1)}, bf16[512,384]{1,0:T(8,128)(2,1)S(1)}, u32[]{:S(2)}, u32[]{:S(2)}) collective-permute-start(bf16[512,384]{1,0:T(8,128)(2,1)S(1)} %collective-permute-done.2), channel_id=1, source_target_pairs={{0,1},{1,2},{2,3},{3,4},{4,5},{5,6},{6,7},{7,8},{8,9},{9,10},{10,1... | collective-permute-start | bytes 1179656 | tf_op jit(solution)/shard_map/ppermute | solution.py:18
  44.4 20.5 %collective-permute-start.5 = (bf16[512,384]{1,0:T(8,128)(2,1)S(1)}, bf16[512,384]{1,0:T(8,128)(2,1)S(1)}, u32[]{:S(2)}, u32[]{:S(2)}) collective-permute-start(bf16[512,384]{1,0:T(8,128)(2,1)S(1)} %collective-permute-done.3), channel_id=1, source_target_pairs={{0,15},{1,0},{2,1},{3,2},{4,3},{5,4},{6,5},{7,6},{8,7},{9,8},{10,9... | collective-permute-start | bytes 1179656 | tf_op jit(solution)/shard_map/ppermute | solution.py:21
  64.8 18.6 %copy-start.2 = (bf16[512,384]{1,0:T(8,128)(2,1)}, bf16[512,384]{1,0:T(8,128)(2,1)S(1)}, u32[]{:S(2)}) copy-start(bf16[512,384]{1,0:T(8,128)(2,1)S(1)} %collective-permute-done.4) | copy-start | bytes 1179652
  64.8 17.4 %collective-permute-start.6 = (bf16[512,384]{1,0:T(8,128)(2,1)S(1)}, bf16[512,384]{1,0:T(8,128)(2,1)S(1)}, u32[]{:S(2)}, u32[]{:S(2)}) collective-permute-start(bf16[512,384]{1,0:T(8,128)(2,1)S(1)} %collective-permute-done.4), channel_id=1, source_target_pairs={{0,1},{1,2},{2,3},{3,4},{4,5},{5,6},{6,7},{7,8},{8,9},{9,10},{10,1... | collective-permute-start | bytes 1179656 | tf_op jit(solution)/shard_map/ppermute | solution.py:18
  64.8 25.4 %collective-permute-start.7 = (bf16[512,384]{1,0:T(8,128)(2,1)S(1)}, bf16[512,384]{1,0:T(8,128)(2,1)S(1)}, u32[]{:S(2)}, u32[]{:S(2)}) collective-permute-start(bf16[512,384]{1,0:T(8,128)(2,1)S(1)} %collective-permute-done.5), channel_id=1, source_target_pairs={{0,15},{1,0},{2,1},{3,2},{4,3},{5,4},{6,5},{7,6},{8,7},{9,8},{10,9... | collective-permute-start | bytes 1179656 | tf_op jit(solution)/shard_map/ppermute | solution.py:21
  82.2 11.8 %collective-permute-start.8 = (bf16[512,384]{1,0:T(8,128)(2,1)S(1)}, bf16[512,384]{1,0:T(8,128)(2,1)}, u32[]{:S(2)}, u32[]{:S(2)}) collective-permute-start(bf16[512,384]{1,0:T(8,128)(2,1)S(1)} %collective-permute-done.6), channel_id=1, source_target_pairs={{0,1},{1,2},{2,3},{3,4},{4,5},{5,6},{6,7},{7,8},{8,9},{9,10},{10,1... | collective-permute-start | bytes 1179656 | tf_op jit(solution)/shard_map/ppermute | solution.py:18
  85.5 10.1 %copy-start.3 = (bf16[512,384]{1,0:T(8,128)(2,1)S(1)}, bf16[512,384]{1,0:T(8,128)(2,1)}, u32[]{:S(2)}) copy-start(bf16[512,384]{1,0:T(8,128)(2,1)} %copy-done.2) | copy-start | bytes 1179652
  85.5 4.0 copy-start.5
  90.3 11.7 %collective-permute-start.9 = (bf16[512,384]{1,0:T(8,128)(2,1)S(1)}, bf16[512,384]{1,0:T(8,128)(2,1)S(1)}, u32[]{:S(2)}, u32[]{:S(2)}) collective-permute-start(bf16[512,384]{1,0:T(8,128)(2,1)S(1)} %collective-permute-done.7), channel_id=1, source_target_pairs={{0,15},{1,0},{2,1},{3,2},{4,3},{5,4},{6,5},{7,6},{8,7},{9,8},{10,9... | collective-permute-start | bytes 1179656 | tf_op jit(solution)/shard_map/ppermute | solution.py:21
  94.0 12.4 %collective-permute-start.10 = (bf16[512,384]{1,0:T(8,128)(2,1)}, bf16[512,384]{1,0:T(8,128)(2,1)S(1)}, u32[]{:S(2)}, u32[]{:S(2)}) collective-permute-start(bf16[512,384]{1,0:T(8,128)(2,1)} %collective-permute-done.8), channel_id=1, source_target_pairs={{0,1},{1,2},{2,3},{3,4},{4,5},{5,6},{6,7},{7,8},{8,9},{9,10},{10,1... | collective-permute-start | bytes 1179656 | tf_op jit(solution)/shard_map/ppermute | solution.py:18
  101.9 12.5 %collective-permute-start.11 = (bf16[512,384]{1,0:T(8,128)(2,1)S(1)}, bf16[512,384]{1,0:T(8,128)(2,1)S(1)}, u32[]{:S(2)}, u32[]{:S(2)}) collective-permute-start(bf16[512,384]{1,0:T(8,128)(2,1)S(1)} %collective-permute-done.9), channel_id=1, source_target_pairs={{0,15},{1,0},{2,1},{3,2},{4,3},{5,4},{6,5},{7,6},{8,7},{9,8},{10,9... | collective-permute-start | bytes 1179656 | tf_op jit(solution)/shard_map/ppermute | solution.py:21
  106.4 12.5 %collective-permute-start.12 = (bf16[512,384]{1,0:T(8,128)(2,1)S(1)}, bf16[512,384]{1,0:T(8,128)(2,1)S(1)}, u32[]{:S(2)}, u32[]{:S(2)}) collective-permute-start(bf16[512,384]{1,0:T(8,128)(2,1)S(1)} %collective-permute-done.10), channel_id=1, source_target_pairs={{0,1},{1,2},{2,3},{3,4},{4,5},{5,6},{6,7},{7,8},{8,9},{9,10},{10,1... | collective-permute-start | bytes 1179656 | tf_op jit(solution)/shard_map/ppermute | solution.py:18
  114.5 12.3 %collective-permute-start.13 = (bf16[512,384]{1,0:T(8,128)(2,1)S(1)}, bf16[512,384]{1,0:T(8,128)(2,1)S(1)}, u32[]{:S(2)}, u32[]{:S(2)}) collective-permute-start(bf16[512,384]{1,0:T(8,128)(2,1)S(1)} %collective-permute-done.11), channel_id=1, source_target_pairs={{0,15},{1,0},{2,1},{3,2},{4,3},{5,4},{6,5},{7,6},{8,7},{9,8},{10,9... | collective-permute-start | bytes 1179656 | tf_op jit(solution)/shard_map/ppermute | solution.py:21
  119.0 12.1 %collective-permute-start.14 = (bf16[512,384]{1,0:T(8,128)(2,1)S(1)}, bf16[512,384]{1,0:T(8,128)(2,1)S(1)}, u32[]{:S(2)}, u32[]{:S(2)}) collective-permute-start(bf16[512,384]{1,0:T(8,128)(2,1)S(1)} %collective-permute-done.12), channel_id=1, source_target_pairs={{0,1},{1,2},{2,3},{3,4},{4,5},{5,6},{6,7},{7,8},{8,9},{9,10},{10,1... | collective-permute-start | bytes 1179656 | tf_op jit(solution)/shard_map/ppermute | solution.py:18
  438.8 84.5 %all-gather.8.cloned.1.call-start = ((), (), s32[]{:S(2)}) async-start(), calls=%async_computation.3 | async-start | bytes 7077888 | tf_op jit(solution)/shard_map/all_gather | solution.py:88
  439.5 197.6 %reduce-scatter.2.cloned.1.call-start = ((), (), s32[]{:S(2)}) async-start(), calls=%async_computation.4 | async-start | bytes 10027008 | tf_op jit(solution)/shard_map/reduce_scatter | solution.py:92
Sparse Core Ops, SparseCore 0:
  9.9 72.8 all-gather.3
  438.9 62.2 all-gather.5
  503.0 20.2 all-gather.7
  525.7 111.4 reduce-scatter.1
